TPU v7x, 256 devices: a whole 4x4x8 slice. The times are simulated.
256 devices in a mesh: dp: 8 (over z), seq: 32 (over x, y, core).
Axes of the slice: x: 4, y: 4, z: 8, core: 2. Of those that a mesh axis runs over, the one named last changes fastest.
Arguments:
- tokens: bfloat16 [128, 4, 2560], P('dp'), may hold values from -6 to 6
- attn_gain: float32 [2560], replicated, may hold values from 0.1 to 1.9
- qkv_weight: bfloat16 [3072, 2560], P(('seq', 'dp'))
- out_weight: bfloat16 [2560, 2560], P(('seq', 'dp')), may hold values from -0.125 to 0.125
- mlp_gain: float32 [2560], replicated, may hold values from 0.1 to 1.9
- gate_up: bfloat16 [2, 7680, 2560], P(None, 'seq'), may hold values from -0.125 to 0.125
- down_weight: bfloat16 [7680, 2560], P('seq'), may hold values from -0.0625 to 0.0625
- kv_pool: bfloat16 [4096, 128, 512], P(('dp', 'seq')), may hold values from -6 to 6
- cache_len: int32 [128], P('dp'), may hold values from 1 to 16384, as said below
- page_table: int32 [128, 16], P('dp'), may hold values from 0 to 511, as said below
Outputs:
- layer_out: bfloat16 [128, 4, 2560], P('dp')
- written_pool: bfloat16 [4096, 128, 512], P(('dp', 'seq'))
Inputs may be any that keep to these rules, and one draw needn't show every extreme that they name: `cache_len`: some request of the whole batch has exactly 16384 cached tokens; lengths under 2048 occur. `page_table`: within the 16 requests of one dp index all entries differ. Slot s lies on seq index s // 16; in every dp index some seq index holds exactly 16 of its pages.
All inputs are finite; a program needn't handle non-finite values.
Results may differ from a plain program's by a relative error of at most 0.018.
Values may be sent and summed in bfloat16 or wider, within the bound.
A program may use at most 128 MiB of HBM per device.

v0:
```python
import jax
import jax.numpy as jnp
from jax import lax
from jax.sharding import PartitionSpec as P

low_fill = -1e30


def rms_norm(values, gains):
    floats = values.astype(jnp.float32)
    return floats * lax.rsqrt(jnp.mean(floats * floats, axis=-1, keepdims=True) + 1e-06) * gains


def rotate(values, positions):
    quarter = values.shape[-1] // 4
    freq_index = jnp.arange(quarter).astype(jnp.float32)
    inverse = 10000.0 ** (-freq_index / quarter)
    angles = positions[..., None] * inverse
    first = values[..., :quarter]
    second = values[..., quarter : 2 * quarter]
    others = values[..., 2 * quarter :]
    cosine = jnp.cos(angles)
    sine = jnp.sin(angles)
    return jnp.concatenate(
        [first * cosine - second * sine, second * cosine + first * sine, others], axis=-1
    )


def body(
    tokens,
    attn_gain,
    qkv_weight,
    out_weight,
    mlp_gain,
    gate_up,
    down_weight,
    kv_pool,
    cache_len,
    page_table,
):
    seq_index = lax.axis_index("seq")
    requests, new_count, model_width = tokens.shape
    slot_count, page_len, pair_width = kv_pool.shape
    head_dim = pair_width // 2
    head_count = out_weight.shape[1] // head_dim
    page_count = page_table.shape[1]
    window = page_count * page_len
    row_count = requests * new_count
    query_rows = new_count * head_count
    split_q = head_count * head_dim
    scale = head_dim ** (-0.5)
    contract = (((1,), (1,)), ((), ()))
    qkv_local, out_local = (
        lax.all_gather(qkv_weight, "dp", axis=0, tiled=True),
        lax.all_gather(out_weight, "dp", axis=0, tiled=True),
    )
    normed = rms_norm(tokens, attn_gain).astype(jnp.bfloat16).reshape(row_count, model_width)
    local_part = lax.dot_general(
        normed, qkv_local, contract, preferred_element_type=jnp.float32
    ).astype(jnp.bfloat16)
    projected = lax.all_gather(local_part, "seq", axis=1, tiled=True).reshape(
        requests, new_count, -1
    )
    positions_int = cache_len[:, None] + jnp.arange(new_count, dtype=jnp.int32)[None, :]
    positions = positions_int.astype(jnp.float32)
    queries = rotate(
        projected[:, :, :split_q]
        .astype(jnp.float32)
        .reshape(requests, new_count, head_count, head_dim),
        positions[:, :, None],
    ).astype(jnp.bfloat16)
    keys_new = rotate(
        projected[:, :, split_q : split_q + head_dim].astype(jnp.float32), positions
    ).astype(jnp.bfloat16)
    values_new = projected[:, :, split_q + head_dim :]
    slot_ids = seq_index * slot_count + jnp.arange(slot_count, dtype=jnp.int32)
    matches = page_table[None, :, :] == slot_ids[:, None, None]
    owners = jnp.any(matches, axis=2)
    in_use = jnp.any(owners, axis=1)
    page_of = jnp.sum(
        jnp.where(matches, jnp.arange(page_count, dtype=jnp.int32)[None, None, :], 0), axis=(1, 2)
    )
    slot_length = jnp.sum(jnp.where(owners, cache_len[None, :], 0), axis=1)
    query_flat = queries.reshape(requests, query_rows * head_dim)
    slot_queries = jnp.dot(
        owners.astype(jnp.bfloat16), query_flat, preferred_element_type=jnp.float32
    )
    slot_queries = slot_queries.astype(jnp.bfloat16).reshape(slot_count, query_rows, head_dim)
    scores = (
        jnp.einsum(
            "pqd,pkd->pqk",
            slot_queries,
            kv_pool[:, :, :head_dim],
            preferred_element_type=jnp.float32,
        )
        * scale
    )
    cycle = page_of[:, None] * page_len + jnp.arange(page_len, dtype=jnp.int32)[None, :]
    key_pos = slot_length[:, None] - 1 - jnp.mod(slot_length[:, None] - 1 - cycle, window)
    query_pos = (
        slot_length[:, None] + (jnp.arange(query_rows, dtype=jnp.int32) // head_count)[None, :]
    )
    visible = (
        in_use[:, None, None]
        & (key_pos >= 0)[:, None, :]
        & (key_pos[:, None, :] > query_pos[:, :, None] - window)
    )
    slot_peak = jnp.max(jnp.where(visible, scores, low_fill), axis=2)
    weights = jnp.where(visible, jnp.exp(scores - slot_peak[:, :, None]), 0.0)
    slot_sum = jnp.sum(weights, axis=2)
    slot_out = jnp.einsum(
        "pqk,pkd->pqd",
        weights.astype(jnp.bfloat16),
        kv_pool[:, :, head_dim:],
        preferred_element_type=jnp.float32,
    )
    request_peak = jnp.max(jnp.where(owners[:, :, None], slot_peak[:, None, :], low_fill), axis=0)
    owner_peak = jnp.max(jnp.where(owners[:, :, None], request_peak[None, :, :], low_fill), axis=1)
    factor = jnp.exp(slot_peak - owner_peak)
    request_sum = jnp.sum(
        jnp.where(owners[:, :, None], (slot_sum * factor)[:, None, :], 0.0), axis=0
    )
    request_out = jnp.einsum(
        "pr,pqd->rqd",
        owners.astype(jnp.float32),
        slot_out * factor[:, :, None],
        precision=lax.Precision.HIGHEST,
    )
    query_block = queries.reshape(requests, query_rows, head_dim)
    new_scores = (
        jnp.einsum("rqd,rud->rqu", query_block, keys_new, preferred_element_type=jnp.float32)
        * scale
    )
    causal = jnp.arange(new_count)[None, :] <= (jnp.arange(query_rows) // head_count)[:, None]
    new_peak = jnp.max(jnp.where(causal[None], new_scores, low_fill), axis=2)
    global_peak = lax.pmax(request_peak, "seq")
    rescale = jnp.exp(request_peak - global_peak)
    old_denominator, weighted = (
        lax.psum((request_sum * rescale).astype(jnp.bfloat16), "seq").astype(jnp.float32),
        lax.psum((request_out * rescale[:, :, None]).astype(jnp.bfloat16), "seq").astype(
            jnp.float32
        ),
    )
    top_peak = jnp.maximum(global_peak, new_peak)
    new_weights = jnp.where(causal[None], jnp.exp(new_scores - top_peak[:, :, None]), 0.0)
    carried = jnp.exp(global_peak - top_peak)
    fresh_sum = jnp.sum(new_weights, axis=2)
    fresh_out = jnp.einsum(
        "rqu,rud->rqd",
        new_weights.astype(jnp.bfloat16),
        values_new,
        preferred_element_type=jnp.float32,
    )
    carried, fresh_sum, fresh_out = (carried, fresh_sum, fresh_out)
    denominator = old_denominator * carried + fresh_sum
    numerator = weighted * carried[:, :, None] + fresh_out
    attended = (
        (numerator / denominator[:, :, None]).astype(jnp.bfloat16).reshape(row_count, split_q)
    )
    heads_part = lax.dot_general(
        attended, out_local, contract, preferred_element_type=jnp.float32
    ).astype(jnp.bfloat16)
    heads_out = lax.all_gather(heads_part, "seq", axis=1, tiled=True)
    residual = (
        tokens.reshape(row_count, model_width).astype(jnp.float32) + heads_out.astype(jnp.float32)
    ).astype(jnp.bfloat16)
    hidden_in = rms_norm(residual, mlp_gain).astype(jnp.bfloat16)
    gate_and_up = jnp.einsum("rd,gfd->grf", hidden_in, gate_up, preferred_element_type=jnp.float32)
    hidden = (jax.nn.gelu(gate_and_up[0], approximate=True) * gate_and_up[1]).astype(jnp.bfloat16)
    partial_sum = jnp.dot(hidden, down_weight, preferred_element_type=jnp.float32)
    full_sum = lax.psum(partial_sum.astype(jnp.bfloat16), "seq").astype(jnp.float32)
    layer_out = (residual.astype(jnp.float32) + full_sum).astype(jnp.bfloat16)
    layer_out = layer_out.reshape(requests, new_count, model_width)
    page_index = jnp.mod(positions_int // page_len, page_count)
    slot_taken = jnp.take_along_axis(page_table, page_index, axis=1)
    local_slot = slot_taken - seq_index * slot_count
    local_slot = jnp.where((local_slot >= 0) & (local_slot < slot_count), local_slot, slot_count)
    offset = jnp.mod(positions_int, page_len)
    new_rows = jnp.concatenate([keys_new, values_new], axis=-1)
    written_pool = kv_pool.at[local_slot, offset].set(new_rows, mode="drop")
    return (layer_out, written_pool)


def solution(mesh):
    in_specs = (
        P("dp", None, None),
        P(),
        P(("seq", "dp"), None),
        P(("seq", "dp"), None),
        P(),
        P(None, "seq", None),
        P("seq", None),
        P(("dp", "seq"), None, None),
        P("dp"),
        P("dp", None),
    )
    out_specs = (P("dp", None, None), P(("dp", "seq"), None, None))
    return jax.shard_map(body, mesh=mesh, in_specs=in_specs, out_specs=out_specs, check_vma=False)
```

profile of v0, /device:TPU:1, one launch (start us, length us, event | category | flops | bytes accessed | tf_op | source)
XLA Modules:
  0.0 415.1 jit_solution(9135690108365068851)
XLA Ops:
  7.2 3.2 copy.131
  10.5 0.6 multiply_power_fusion
  11.1 24.0 %all-gather = bf16[8,12,2560]{2,1,0:T(8,128)(2,1)S(1)} all-gather(bf16[1,12,2560]{2,1,0:T(8,128)(2,1)S(1)} %bitcast.64), channel_id=1, replica_groups=mesh['dp'=8,'seq'=32] {'dp'}, dimensions={0}, use_global_device_ids=true | all-gather | bytes 552960 | tf_op jit(solution)/shard_map/all_gather | solution.py:54
  35.1 0.9 reshape.604
  36.0 0.3 multiply_reduce_fusion
  36.3 0.2 multiply_convert_fusion
  36.6 1.3 fusion.1
  37.9 31.8 %all-gather.1 = bf16[32,96,64]{1,2,0:T(8,128)(2,1)S(1)} all-gather(bf16[1,96,64]{1,2,0:T(8,128)(2,1)S(1)} %fusion.1), channel_id=1, replica_groups=mesh['dp'=8,'seq'=32] {'seq'}, dimensions={0}, use_global_device_ids=true | all-gather | bytes 405504 | tf_op jit(solution)/shard_map/all_gather | solution.py:61
  69.7 0.3 copy.91
  70.1 0.7 reshape.606
  70.8 0.2 reshape.581
  71.0 0.1 slice.62
  71.1 1.0 compare_reduce_fusion
  72.1 1.0 fusion.30
  73.1 0.5 and_select_fusion
  73.6 0.6 copy_convert_fusion.1
  74.3 0.5 add_convert_fusion.2
  74.8 0.9 copy_convert_fusion
  75.7 1.2 reshape.589
  77.0 1.0 subtract_convert_fusion.1
  78.1 0.2 subtract_convert_fusion
  78.4 0.3 pad_maximum_fusion
  78.7 0.4 copy-done.7
  79.2 0.9 convert_element_type.110
  80.1 0.1 select_reduce_fusion.5
  80.2 1.2 convolution_convert_fusion
  81.8 2.4 select_reduce_fusion
  84.3 0.1 select_reduce_fusion.3
  84.4 0.1 select_reduce_fusion.2
  84.5 63.2 %pmax.7 = f32[16,40]{1,0:T(8,128)S(1)} all-reduce(f32[16,40]{1,0:T(8,128)S(1)} %select_reduce_fusion.3), channel_id=1, replica_groups=mesh['dp'=8,'seq'=32] {'seq'}, use_global_device_ids=true, to_apply=%region_8.9 | all-reduce | flops 640 | bytes 5120 | tf_op jit(solution)/shard_map/pmax | solution.py:136
  147.9 1.5 fusion.22
  149.4 0.1 select_reduce_fusion.1
  149.7 0.6 convolution_multiply_fusion.1
  150.4 0.3 select_reduce_fusion.4
  150.7 0.7 copy.96
  151.4 2.1 fusion
  153.6 0.9 reshape.587
  154.4 0.7 shift-left_or_fusion
  155.2 65.4 %psum.22 = bf16[16,40]{1,0:T(8,128)(2,1)S(1)} all-reduce(bf16[16,40]{1,0:T(8,128)(2,1)S(1)} %get-tuple-element.8), channel_id=1, replica_groups=mesh['dp'=8,'seq'=32] {'seq'}, use_global_device_ids=true, to_apply=%region_13.14 | all-reduce | flops 640 | bytes 2560 | tf_op jit(solution)/shard_map/psum | solution.py:139
  220.6 0.6 fusion.52
  221.3 0.7 copy.106
  221.9 0.7 copy.108
  222.6 20.4 %all-gather.2 = bf16[8,10,2560]{2,1,0:T(8,128)(2,1)S(1)} all-gather(bf16[1,10,2560]{2,1,0:T(8,128)(2,1)} %bitcast.65), channel_id=1, replica_groups=mesh['dp'=8,'seq'=32] {'dp'}, dimensions={0}, use_global_device_ids=true | all-gather | bytes 460800 | tf_op jit(solution)/shard_map/all_gather | solution.py:55
  243.1 0.9 reshape.608
  244.1 0.6 reshape.598
  244.8 0.8 gather_fusion
  245.7 0.1 copy-done.12
  245.8 0.9 fusion.41
  246.7 16.8 %all-reduce.3.cloned.1.call-done = bf16[16,40,256]{2,0,1:T(8,128)(2,1)} async-done(((bf16[16,40,256]{2,0,1:T(8,128)(2,1)}), bf16[16,40,256]{2,0,1:T(8,128)(2,1)}) %all-reduce.3.cloned.1.call-update) | async-done | bytes 327696 | tf_op jit(solution)/shard_map/psum | solution.py:140
  263.5 1.3 fusion.11
  264.8 0.1 copy.109
  264.9 0.4 reshape.585
  265.3 1.3 fusion.2
  266.5 23.5 %all-gather.3 = bf16[32,80,64]{1,2,0:T(8,128)(2,1)S(1)} all-gather(bf16[1,80,64]{1,2,0:T(8,128)(2,1)S(1)} %fusion.2), channel_id=1, replica_groups=mesh['dp'=8,'seq'=32] {'seq'}, dimensions={0}, use_global_device_ids=true | all-gather | bytes 337920 | tf_op jit(solution)/shard_map/all_gather | solution.py:163
  290.1 0.3 copy.110
  290.4 1.4 reshape.611
  291.9 1.6 fusion.5
  293.5 0.9 convolution_bitcast_fusion
  294.4 1.1 convolution_convert_fusion.1
  295.5 0.1 fusion.59
  295.7 7.9 %scatter_fusion = bf16[16,128,512]{2,1,0:T(8,128)(2,1)} fusion(bf16[16,128,512]{2,1,0:T(8,128)(2,1)} %copy.131, s32[64]{0:T(128)S(1)} %reshape.596, bf16[64,512]{1,0:T(8,128)(2,1)S(1)} %copy-done.15), kind=kCustom, calls=%fused_computation.1 | custom fusion | bytes 197120 | tf_op jit(solution)/shard_map/scatter | solution.py:180
  303.6 102.8 %all-reduce.5.cloned.1.call-done = bf16[64,2560]{1,0:T(8,128)(2,1)} async-done(((bf16[64,2560]{1,0:T(8,128)(2,1)}), bf16[64,2560]{1,0:T(8,128)(2,1)}) %all-reduce.5.cloned.1.call-update) | async-done | bytes 327696 | tf_op jit(solution)/shard_map/psum | solution.py:171
  406.4 1.0 fusion.8
  407.5 0.8 reshape.586
  (92 shorter events, 1.5 us)
Async XLA Ops:
  7.2 286.3 %copy-start = (bf16[2,240,2560]{2,1,0:T(8,128)(2,1)S(1)}, bf16[2,240,2560]{2,1,0:T(8,128)(2,1)}, u32[]{:S(2)}) copy-start(bf16[2,240,2560]{2,1,0:T(8,128)(2,1)} %param.15) | copy-start | bytes 7372804
  7.2 28.8 %copy-start.3 = (bf16[16,4,2560]{2,1,0:T(4,128)(2,1)S(1)}, bf16[16,4,2560]{2,1,0:T(4,128)(2,1)}, u32[]{:S(2)}) copy-start(bf16[16,4,2560]{2,1,0:T(4,128)(2,1)} %param.10) | copy-start | bytes 983044
  7.2 3.9 copy-start.16
  7.2 256.3 %all-reduce.3.cloned.1.call-start = ((), (), s32[]{:S(2)}) async-start(), calls=%async_computation | async-start | bytes 655360 | tf_op jit(solution)/shard_map/psum | solution.py:140
  10.5 25.8 %copy-start.22 = (f32[2560]{0:T(1024)S(1)}, f32[2560]{0:T(1024)}, u32[]{:S(2)}) copy-start(f32[2560]{0:T(1024)} %param.11) | copy-start | bytes 30724
  37.9 33.2 %copy-start.1 = (s32[16,16]{1,0:T(8,128)S(1)}, s32[16,16]{1,0:T(8,128)}, u32[]{:S(2)}) copy-start(s32[16,16]{1,0:T(8,128)} %param.19) | copy-start | bytes 3076
  37.9 36.3 %copy-start.23 = (s32[16]{0:T(128)S(1)}, s32[16]{0:T(128)}, u32[]{:S(2)}) copy-start(s32[16]{0:T(128)} %param.18) | copy-start | bytes 196
  70.9 3.9 copy-start.11
  77.0 1.3 copy-start.5
  78.3 0.7 copy-start.7
  78.3 0.8 copy-start.9
  78.4 3.2 copy-start.27
  78.4 3.3 copy-start.26
  78.4 3.4 copy-start.28
  79.2 68.5 %copy-start.10 = (bf16[16,4,10,64]{3,2,0,1:T(8,128)(2,1)S(1)}, bf16[16,4,10,64]{3,2,0,1:T(8,128)(2,1)}, u32[]{:S(2)}) copy-start(bf16[16,4,10,64]{3,2,0,1:T(8,128)(2,1)} %copy-done.9) | copy-start | bytes 245764
  80.1 67.6 %copy-start.8 = (bf16[16,4,10,64]{3,2,0,1:T(8,128)(2,1)S(1)}, bf16[16,4,10,64]{3,2,0,1:T(8,128)(2,1)}, u32[]{:S(2)}) copy-start(bf16[16,4,10,64]{3,2,0,1:T(8,128)(2,1)} %copy-done.7) | copy-start | bytes 245764
  80.2 67.6 %copy-start.6 = (bf16[16,4,10,128]{3,2,0,1:T(8,128)(2,1)S(1)}, bf16[16,4,10,128]{3,2,0,1:T(8,128)(2,1)}, u32[]{:S(2)}) copy-start(bf16[16,4,10,128]{3,2,0,1:T(8,128)(2,1)} %copy-done.5) | copy-start | bytes 491524
  147.7 2.0 copy-start.2
  147.7 2.0 copy-start.13
  147.8 2.6 slice-start
  147.9 2.8 copy-start.25
  149.6 1.1 copy-start.17
  149.6 1.1 copy-start.19
  149.7 3.8 copy-start.4
  151.4 92.6 %slice-start.1 = ((bf16[16,4,3072]{2,1,0:T(4,128)(2,1)}), bf16[16,4,384]{2,1,0:T(4,128)(2,1)S(1)}, s32[]{:S(2)}) async-start(bf16[16,4,3072]{2,1,0:T(4,128)(2,1)} %copy-done.11), calls=%async_computation.3 | async-start | bytes 98304 | tf_op jit(solution)/shard_map/slice | solution.py:21
  153.5 90.5 %copy-start.18 = (bf16[16,4,64]{2,1,0:T(4,128)(2,1)S(1)}, bf16[16,4,64]{2,1,0:T(4,128)(2,1)}, u32[]{:S(2)}) copy-start(bf16[16,4,64]{2,1,0:T(4,128)(2,1)} %copy-done.17) | copy-start | bytes 24580
  153.5 90.5 %copy-start.20 = (bf16[16,4,64]{2,1,0:T(4,128)(2,1)S(1)}, bf16[16,4,64]{2,1,0:T(4,128)(2,1)}, u32[]{:S(2)}) copy-start(bf16[16,4,64]{2,1,0:T(4,128)(2,1)} %copy-done.19) | copy-start | bytes 24580
  153.5 252.9 %all-reduce.5.cloned.1.call-start = ((), (), s32[]{:S(2)}) async-start(), calls=%async_computation.1 | async-start | bytes 655360 | tf_op jit(solution)/shard_map/psum | solution.py:171
  244.8 1.0 copy-start.12
  290.1 3.4 copy-start.21
  291.9 2.5 copy-start.14
  293.5 2.0 copy-start.24
  293.5 2.2 copy-start.15
Sparse Core Ops, SparseCore 0:
  153.6 109.8 all-reduce.2
  295.6 110.8 all-reduce.4
where the time goes:
time: 416 us; the launch traced here: 415 us
  blocking collectives  228 us (55%)
  waiting for transfers between devices  120 us (29%)
  local copies, waits for them, and re-layouts  25.4 us (6%)
  other arithmetic  14.8 us (4%)
  between operations  14.7 us (4%)
  matrix products  12 us (3%)
    psum x1, waiting for transfers between devices, body(): lax.psum(partial_sum.astype(jnp.bfloat16), 'seq').astype(jnp.float32)  103 us
    psum x1, blocking collectives, body(): lax.psum((request_sum * rescale).astype(jnp.bfloat16), 'seq')  65.4 us
    pmax x1, blocking collectives, body(): global_peak = lax.pmax(request_peak, 'seq')  63.2 us
    all_gather x1, blocking collectives, body(): lax.all_gather(local_part, 'seq', axis=1, tiled=True)  31.8 us
    all_gather x1, blocking collectives, body(): lax.all_gather(qkv_weight, 'dp', axis=0, tiled=True)  24 us
    all_gather x1, blocking collectives, body(): heads_out = lax.all_gather(heads_part, 'seq', axis=1, tiled=True)  23.5 us
    all_gather x1, blocking collectives, body(): lax.all_gather(out_weight, 'dp', axis=0, tiled=True)  20.4 us
    psum x1, waiting for transfers between devices, body(): lax.psum((request_out * rescale[:, :, None]).astype(jnp.bfloat16), 'seq')  16.8 us
  transfers between devices with their start and end apart: 2, of which 2 were waited for; matrix products, arithmetic and copies ran while one was open for 4% of the time, Pallas kernels for 0%

commit v1 on v0

--- a/solution.py
+++ b/solution.py
@@ -168,7 +168,8 @@
     gate_and_up = jnp.einsum("rd,gfd->grf", hidden_in, gate_up, preferred_element_type=jnp.float32)
     hidden = (jax.nn.gelu(gate_and_up[0], approximate=True) * gate_and_up[1]).astype(jnp.bfloat16)
     partial_sum = jnp.dot(hidden, down_weight, preferred_element_type=jnp.float32)
-    full_sum = lax.psum(partial_sum.astype(jnp.bfloat16), "seq").astype(jnp.float32)
+    proceed_rounds = lambda mine_x: lax.all_gather(mine_x, "seq").sum(axis=0)
+    full_sum = proceed_rounds(partial_sum.astype(jnp.bfloat16)).astype(jnp.float32)
     layer_out = (residual.astype(jnp.float32) + full_sum).astype(jnp.bfloat16)
     layer_out = layer_out.reshape(requests, new_count, model_width)
     page_index = jnp.mod(positions_int // page_len, page_count)

time: 416 us -> 371 us (0.89)
  waiting for transfers between devices: 120 us -> 64.9 us
  blocking collectives: 228 us -> 234 us
  other arithmetic: 14.8 us -> 19.3 us
    psum x1 -> x0, waiting for transfers between devices: 103 us -> none  [body(): lax.psum(partial_sum.astype(jnp.bfloat16), 'seq').astype(jnp.float32)]
    all_gather x0 -> x1, waiting for transfers between devices: none -> 51.9 us  [body(): proceed_rounds = lambda mine_x: lax.all_gather(mine_x, 'seq').sum(axis=0)]
    reduce_sum x0 -> x1, other arithmetic: none -> 5.69 us  [body(): proceed_rounds = lambda mine_x: lax.all_gather(mine_x, 'seq').sum(axis=0)]
    psum x1, blocking collectives: 65.4 us -> 70.6 us  [body(): lax.psum((request_sum * rescale).astype(jnp.bfloat16), 'seq')]
where the time goes in v1:
time: 371 us; the launch traced here: 370 us
  blocking collectives  234 us (63%)
  waiting for transfers between devices  64.9 us (17%)
  local copies, waits for them, and re-layouts  25.5 us (7%)
  other arithmetic  19.3 us (5%)
  between operations  14.7 us (4%)
  matrix products  11.9 us (3%)
    psum x1, blocking collectives, body(): lax.psum((request_sum * rescale).astype(jnp.bfloat16), 'seq')  70.6 us
    pmax x1, blocking collectives, body(): global_peak = lax.pmax(request_peak, 'seq')  63.2 us
    all_gather x1, waiting for transfers between devices, body(): proceed_rounds = lambda mine_x: lax.all_gather(mine_x, 'seq').sum(axis=0)  51.9 us
    all_gather x1, blocking collectives, body(): lax.all_gather(local_part, 'seq', axis=1, tiled=True)  31.8 us
    all_gather x1, blocking collectives, body(): lax.all_gather(qkv_weight, 'dp', axis=0, tiled=True)  24 us
    all_gather x1, blocking collectives, body(): heads_out = lax.all_gather(heads_part, 'seq', axis=1, tiled=True)  23.5 us
    all_gather x1, blocking collectives, body(): lax.all_gather(out_weight, 'dp', axis=0, tiled=True)  20.7 us
    psum x1, waiting for transfers between devices, body(): lax.psum((request_out * rescale[:, :, None]).astype(jnp.bfloat16), 'seq')  13 us
  transfers between devices with their start and end apart: 2, of which 2 were waited for; matrix products, arithmetic and copies ran while one was open for 4% of the time, Pallas kernels for 0%

profile of v1, /device:TPU:1, one launch (start us, length us, event | category | flops | bytes accessed | tf_op | source)
XLA Modules:
  0.0 370.2 jit_solution(3798607268583272912)
XLA Ops:
  7.3 3.2 copy.130
  10.5 0.6 and_select_fusion
  11.1 0.5 multiply_power_fusion
  11.6 0.4 fusion.30
  12.1 1.0 compare_reduce_fusion
  13.1 0.3 multiply_reduce_fusion
  13.3 0.2 multiply_convert_fusion
  13.7 24.0 %all-gather.1 = bf16[8,12,2560]{2,1,0:T(8,128)(2,1)S(1)} all-gather(bf16[1,12,2560]{2,1,0:T(8,128)(2,1)S(1)} %bitcast.67), channel_id=1, replica_groups=mesh['dp'=8,'seq'=32] {'dp'}, dimensions={0}, use_global_device_ids=true | all-gather | bytes 552960 | tf_op jit(solution)/shard_map/all_gather | solution.py:54
  37.7 0.9 reshape.605
  38.6 1.3 fusion.1
  39.9 31.8 %all-gather.2 = bf16[32,96,64]{1,2,0:T(8,128)(2,1)S(1)} all-gather(bf16[1,96,64]{1,2,0:T(8,128)(2,1)S(1)} %fusion.1), channel_id=1, replica_groups=mesh['dp'=8,'seq'=32] {'seq'}, dimensions={0}, use_global_device_ids=true | all-gather | bytes 405504 | tf_op jit(solution)/shard_map/all_gather | solution.py:61
  71.7 0.3 copy.91
  72.0 0.7 reshape.607
  72.8 0.2 reshape.581
  73.0 0.1 slice.62
  73.1 0.6 copy_convert_fusion.1
  73.7 0.9 copy_convert_fusion
  74.6 1.2 reshape.589
  76.0 1.6 subtract_convert_fusion.1
  77.6 0.2 subtract_convert_fusion
  77.8 0.7 copy.97
  78.6 0.3 pad_maximum_fusion
  78.9 0.7 copy.99
  79.6 0.6 iota_compare_fusion
  80.2 0.1 select_reduce_fusion.5
  80.6 0.2 convert_element_type.112
  80.8 0.2 convolution_convert_fusion
  81.1 1.8 select_reduce_fusion
  82.9 0.1 select_reduce_fusion.3
  83.0 63.2 %pmax.7 = f32[16,40]{1,0:T(8,128)S(1)} all-reduce(f32[16,40]{1,0:T(8,128)S(1)} %select_reduce_fusion.3), channel_id=1, replica_groups=mesh['dp'=8,'seq'=32] {'seq'}, use_global_device_ids=true, to_apply=%region_8.9 | all-reduce | flops 640 | bytes 5120 | tf_op jit(solution)/shard_map/pmax | solution.py:136
  146.2 0.1 select_reduce_fusion.2
  146.3 0.7 copy.104
  147.3 0.4 fusion.22
  147.7 0.1 select_reduce_fusion.1
  147.8 1.6 select_reduce_fusion.4
  149.4 0.6 multiply_convert_fusion.1
  150.0 0.7 copy.96
  150.7 1.7 convolution_multiply_fusion.1
  152.4 2.1 fusion
  154.6 0.9 reshape.587
  155.5 20.7 %all-gather.3 = bf16[8,10,2560]{2,1,0:T(8,128)(2,1)S(1)} all-gather(bf16[1,10,2560]{2,1,0:T(8,128)(2,1)} %bitcast.68), channel_id=1, replica_groups=mesh['dp'=8,'seq'=32] {'dp'}, dimensions={0}, use_global_device_ids=true | all-gather | bytes 460800 | tf_op jit(solution)/shard_map/all_gather | solution.py:55
  176.2 0.9 reshape.609
  177.1 70.6 %psum.15 = bf16[16,40]{1,0:T(8,128)(2,1)S(1)} all-reduce(bf16[16,40]{1,0:T(8,128)(2,1)} %get-tuple-element.8), channel_id=1, replica_groups=mesh['dp'=8,'seq'=32] {'seq'}, use_global_device_ids=true, to_apply=%region_13.14 | all-reduce | flops 640 | bytes 2560 | tf_op jit(solution)/shard_map/psum | solution.py:139
  247.7 0.7 fusion.52
  248.4 0.7 multiply_add_fusion
  249.1 0.7 copy.108
  249.8 0.7 copy.106
  250.5 1.0 fusion.41
  251.5 13.0 %all-reduce.2.cloned.1.call-done = bf16[16,40,256]{2,0,1:T(8,128)(2,1)} async-done(((bf16[16,40,256]{2,0,1:T(8,128)(2,1)}), bf16[16,40,256]{2,0,1:T(8,128)(2,1)}) %all-reduce.2.cloned.1.call-update) | async-done | bytes 327696 | tf_op jit(solution)/shard_map/psum | solution.py:140
  264.5 1.3 fusion.11
  265.9 0.4 reshape.585
  266.3 0.3 fusion.2
  266.6 23.5 %all-gather.4 = bf16[32,80,64]{1,2,0:T(8,128)(2,1)S(1)} all-gather(bf16[1,80,64]{1,2,0:T(8,128)(2,1)S(1)} %fusion.2), channel_id=1, replica_groups=mesh['dp'=8,'seq'=32] {'seq'}, dimensions={0}, use_global_device_ids=true | all-gather | bytes 337920 | tf_op jit(solution)/shard_map/all_gather | solution.py:163
  290.1 0.3 copy.110
  290.4 1.4 reshape.612
  291.9 1.6 fusion.5
  293.5 0.9 convolution_bitcast_fusion
  294.4 1.1 convolution_convert_fusion.1
  295.7 0.8 gather_fusion
  296.6 0.1 fusion.59
  296.9 7.9 %scatter_fusion = bf16[16,128,512]{2,1,0:T(8,128)(2,1)} fusion(bf16[16,128,512]{2,1,0:T(8,128)(2,1)} %copy.130, s32[64]{0:T(128)S(1)} %reshape.596, bf16[64,512]{1,0:T(8,128)(2,1)S(1)} %reshape.598), kind=kCustom, calls=%fused_computation.1 | custom fusion | bytes 197120 | tf_op jit(solution)/shard_map/scatter | solution.py:181
  304.9 51.9 %all-gather.7.cloned.1.call-done = bf16[2048,2560]{1,0:T(8,128)(2,1)} async-done(((bf16[64,2560]{1,0:T(8,128)(2,1)}), bf16[2048,2560]{1,0:T(8,128)(2,1)}) %all-gather.7.cloned.1.call-update) | async-done | bytes 10485776 | tf_op jit(solution)/shard_map/all_gather | solution.py:171
  356.7 5.7 %reduce_sum.82 = bf16[64,2560]{1,0:T(8,128)(2,1)S(1)} reduce(bf16[32,64,2560]{2,1,0:T(8,128)(2,1)} %bitcast.60, bf16[]{:T(256)} %constant.120.clone.1), dimensions={0}, to_apply=%region_16.17 | reduce | flops 5079040 | bytes 10813442 | tf_op jit(solution)/shard_map/reduce_sum | solution.py:171
  362.5 0.8 reshape.586
  (85 shorter events, 1.6 us)
Async XLA Ops:
  7.2 286.3 %copy-start = (bf16[2,240,2560]{2,1,0:T(8,128)(2,1)S(1)}, bf16[2,240,2560]{2,1,0:T(8,128)(2,1)}, u32[]{:S(2)}) copy-start(bf16[2,240,2560]{2,1,0:T(8,128)(2,1)} %param.15) | copy-start | bytes 7372804
  7.2 5.9 %copy-start.2 = (bf16[16,4,2560]{2,1,0:T(4,128)(2,1)S(1)}, bf16[16,4,2560]{2,1,0:T(4,128)(2,1)}, u32[]{:S(2)}) copy-start(bf16[16,4,2560]{2,1,0:T(4,128)(2,1)} %param.10) | copy-start | bytes 983044
  7.2 6.1 %copy-start.19 = (f32[2560]{0:T(1024)S(1)}, f32[2560]{0:T(1024)}, u32[]{:S(2)}) copy-start(f32[2560]{0:T(1024)} %param.11) | copy-start | bytes 30724
  7.2 6.5 %copy-start.12 = (bf16[12,2560]{1,0:T(8,128)(2,1)S(1)}, bf16[12,2560]{1,0:T(8,128)(2,1)}, u32[]{:S(2)}) copy-start(bf16[12,2560]{1,0:T(8,128)(2,1)} %param.12) | copy-start | bytes 184324
  7.2 4.4 %copy-start.1 = (s32[16,16]{1,0:T(8,128)S(1)}, s32[16,16]{1,0:T(8,128)}, u32[]{:S(2)}) copy-start(s32[16,16]{1,0:T(8,128)} %param.19) | copy-start | bytes 3076
  7.2 257.3 %all-reduce.2.cloned.1.call-start = ((), (), s32[]{:S(2)}) async-start(), calls=%async_computation | async-start | bytes 655360 | tf_op jit(solution)/shard_map/psum | solution.py:140
  13.1 134.6 %copy-start.11 = (pred[16,16]{1,0:T(8,128)(4,1)}, pred[16,16]{1,0:T(8,128)(4,1)S(1)}, u32[]{:S(2)}) copy-start(pred[16,16]{1,0:T(8,128)(4,1)S(1)} %get-tuple-element.3) | copy-start | bytes 772
  39.9 33.2 %copy-start.20 = (s32[16]{0:T(128)S(1)}, s32[16]{0:T(128)}, u32[]{:S(2)}) copy-start(s32[16]{0:T(128)} %param.18) | copy-start | bytes 196
  72.9 0.8 copy-start.4
  72.9 3.0 copy-start.23
  77.6 2.0 copy-start.24
  77.6 2.8 copy-start.22
  80.8 66.3 %copy-start.8 = (bf16[16,4,10,64]{3,0,2,1:T(8,128)(2,1)S(1)}, bf16[16,4,10,64]{3,0,2,1:T(8,128)(2,1)}, u32[]{:S(2)}) copy-start(bf16[16,4,10,64]{3,0,2,1:T(8,128)(2,1)} %copy.97) | copy-start | bytes 245764
  80.8 66.3 %copy-start.9 = (bf16[16,4,10,128]{3,0,2,1:T(8,128)(2,1)S(1)}, bf16[16,4,10,128]{3,0,2,1:T(8,128)(2,1)}, u32[]{:S(2)}) copy-start(bf16[16,4,10,128]{3,0,2,1:T(8,128)(2,1)} %copy.99) | copy-start | bytes 491524
  81.1 66.7 %slice-start = ((bf16[16,4,3072]{2,1,0:T(4,128)(2,1)}), bf16[16,4,128]{2,1,0:T(4,128)(2,1)S(1)}, s32[]{:S(2)}) async-start(bf16[16,4,3072]{2,1,0:T(4,128)(2,1)} %copy-done.4), calls=%async_computation.2 | async-start | bytes 32768 | tf_op jit(solution)/shard_map/slice | solution.py:21
  146.2 4.5 %copy-start.13 = (f32[16,40]{1,0:T(8,128)}, f32[16,40]{1,0:T(8,128)S(1)}, u32[]{:S(2)}) copy-start(f32[16,40]{1,0:T(8,128)S(1)} %pmax.7) | copy-start | bytes 7684
  147.1 3.6 copy-start.14
  147.1 3.0 copy-start.16
  147.8 6.8 %copy-start.3 = (bf16[16,4,2560]{2,1,0:T(4,128)(2,1)S(1)}, bf16[16,4,2560]{2,1,0:T(4,128)(2,1)}, u32[]{:S(2)}) copy-start(bf16[16,4,2560]{2,1,0:T(4,128)(2,1)} %param.10) | copy-start | bytes 983044
  152.4 95.3 %copy-start.10 = (f32[16,40,4]{1,2,0:T(4,128)S(1)}, f32[16,40,4]{1,2,0:T(4,128)}, u32[]{:S(2)}) copy-start(f32[16,40,4]{1,2,0:T(4,128)} %get-tuple-element.22) | copy-start | bytes 30724
  152.4 98.1 %copy-start.5 = (bf16[16,4,3072]{2,1,0:T(4,128)(2,1)S(1)}, bf16[16,4,3072]{2,1,0:T(4,128)(2,1)}, u32[]{:S(2)}) copy-start(bf16[16,4,3072]{2,1,0:T(4,128)(2,1)} %copy-done.4) | copy-start | bytes 1179652
  154.5 202.2 %all-gather.7.cloned.1.call-start = ((), (), s32[]{:S(2)}) async-start(), calls=%async_computation.1 | async-start | bytes 10813440 | tf_op jit(solution)/shard_map/all_gather | solution.py:171
  251.5 14.8 %copy-start.6 = (bf16[80,2560]{1,0:T(8,128)(2,1)S(1)}, bf16[80,2560]{1,0:T(8,128)(2,1)}, u32[]{:S(2)}) copy-start(bf16[80,2560]{1,0:T(8,128)(2,1)} %reshape.609) | copy-start | bytes 1228804
  290.1 3.4 copy-start.18
  291.9 2.5 copy-start.7
  293.5 2.0 copy-start.21
  295.7 1.1 slice-start.1
  295.7 1.1 copy-start.15
  295.7 1.1 copy-start.17
Sparse Core Ops, SparseCore 0:
  154.6 109.8 all-reduce.1
  295.6 61.1 all-gather.6
